TPU v7x, 512 devices: a whole 4x4x16 slice. The times are simulated.
512 devices in a mesh: ctx: 32 (over y, x, z_hi), head: 16 (over z_lo, core).
Axes of the slice: x: 4, y: 4, z: 16 (z_hi: 2, z_lo: 8; z = z_hi * 8 + z_lo), core: 2. Of those that a mesh axis runs over, the one named last changes fastest.
Arguments:
- tokens: bfloat16 [14336, 5376], P('ctx'), may hold values from -6 to 6
- w_query: bfloat16 [5376, 4096], P('ctx', 'head')
- key_weight: bfloat16 [5376, 2048], P('ctx', 'head')
- value_weight: bfloat16 [5376, 2048], P('ctx', 'head'), may hold values from -0.078125 to 0.078125
- query_gain: float32 [128], replicated, may hold values from 0.5 to 16
- key_gain: float32 [128], replicated, may hold values from 0.5 to 16
Outputs:
- attended: bfloat16 [14336, 4096], P('ctx', 'head')
All inputs are finite; a program needn't handle non-finite values.
Results may differ from a plain program's by a relative error of at most 0.025.
Values may be sent and summed in bfloat16 or wider, within the bound.
No kernel may reach another device: no remote copies, remote signals or barrier semaphores. Data moves between devices by JAX's collectives and lax.ppermute only.
A program may use at most 64 MiB of HBM per device.

v0:
```python
import jax
import jax.numpy as jnp
from jax import lax
from jax.sharding import Mesh
from jax.sharding import PartitionSpec as P

WINDOW = 1024
PLANE = ("y", "x")
CTX = ("y", "x", "zh")
HEAD = ("zl", "core")
query_scale = 168.0 ** (-0.5)


def normalize(values, gain):
    return values * lax.rsqrt(jnp.mean(values * values, axis=-1, keepdims=True) + 1e-06) * gain


def rotate(values, position):
    half = values.shape[-1] // 2
    expo = jnp.arange(half, dtype=jnp.float32) * (2.0 / values.shape[-1])
    freq = jnp.power(jnp.float32(10000.0), -expo)
    angle = position[:, None] * freq[None, :]
    cosine = jnp.cos(angle)[:, None, :]
    sine = jnp.sin(angle)[:, None, :]
    first = values[..., :half]
    second = values[..., half:]
    return jnp.concatenate(
        [first * cosine - second * sine, second * cosine + first * sine], axis=-1
    )


def from_behind(block, distance):
    count = lax.axis_size(CTX)
    return lax.ppermute(block, CTX, [(i - distance, i) for i in range(distance, count)])


def on_device(tokens, w_query, key_weight, value_weight, query_gain, key_gain):
    row_count = tokens.shape[0]
    head_size = query_gain.shape[0]
    plane = lax.axis_size(PLANE)
    q_width = w_query.shape[1]
    kv_width = 2 * head_size
    mine = jnp.concatenate([key_weight, value_weight, w_query], axis=1)
    pair = lax.all_gather(mine, "zh", axis=0, tiled=True)
    pair_kv = pair[:, :kv_width]
    pair_q = pair[:, kv_width:]
    all_q = lax.all_gather(pair_q, PLANE, axis=0, tiled=True)
    all_kv = lax.all_to_all(
        jnp.broadcast_to(pair_kv[None], (plane,) + pair_kv.shape), PLANE, 0, 0, tiled=True
    ).reshape(-1, kv_width)
    offset = lax.axis_index(CTX) * row_count
    local_pos = offset + jnp.arange(row_count, dtype=jnp.int32)
    position = local_pos.astype(jnp.float32)
    kv_sum = jnp.dot(tokens, all_kv, preferred_element_type=jnp.float32)
    keys = rotate(normalize(kv_sum[:, None, :head_size], key_gain), position)[:, 0]
    kv = jnp.concatenate(
        [keys.astype(jnp.bfloat16), kv_sum[:, head_size:].astype(jnp.bfloat16)], axis=1
    )
    reach = WINDOW - 1
    hop_count = (reach + row_count - 1) // row_count
    needed = [min(row_count, reach - distance * row_count) for distance in range(hop_count)]
    sizes = [-(-rows // 16) * 16 for rows in needed]
    received = [
        from_behind(kv[row_count - size :], distance + 1) for distance, size in enumerate(sizes)
    ]
    before = sum(sizes)
    all_keys_values = jnp.concatenate(received[::-1] + [kv], axis=0)
    key_pos = offset - before + jnp.arange(before + row_count, dtype=jnp.int32)
    query_sum = jnp.dot(tokens, all_q, preferred_element_type=jnp.float32)
    queries = rotate(
        normalize(query_sum.reshape(row_count, 2, head_size), query_gain), position
    ).astype(jnp.bfloat16)
    allowed = (
        (key_pos[None, :] <= local_pos[:, None])
        & (key_pos[None, :] > local_pos[:, None] - WINDOW)
        & (key_pos[None, :] >= 0)
    )
    scores = (
        jnp.einsum(
            "bgd,cd->gbc",
            queries,
            all_keys_values[:, :head_size],
            preferred_element_type=jnp.float32,
        )
        * query_scale
    )
    scores = jnp.where(allowed[None], scores, jnp.float32(-1e30))
    top = jnp.max(scores, axis=-1, keepdims=True)
    weights = jnp.exp(scores - top)
    probs = (weights / jnp.sum(weights, axis=-1, keepdims=True)).astype(jnp.bfloat16)
    mixed = jnp.einsum(
        "gbc,cd->bgd", probs, all_keys_values[:, head_size:], preferred_element_type=jnp.float32
    )
    return mixed.reshape(row_count, q_width).astype(jnp.bfloat16)


def solution(mesh):
    split = Mesh(mesh.devices.reshape(4, 4, 2, 8, 2), CTX + HEAD)
    placed = (P(CTX, None), P(CTX, HEAD), P(CTX, HEAD), P(CTX, HEAD), P(), P())
    return jax.shard_map(
        on_device, mesh=split, in_specs=placed, out_specs=P(CTX, HEAD), check_vma=False
    )
```

profile of v0, /device:TPU:50, one launch (start us, length us, event | category | flops | bytes accessed | tf_op | source)
XLA Modules:
  0.0 148.6 jit_solution(11865930825600269100)
XLA Ops:
  6.5 0.0 all-gather.2.cloned.1.call-start
  6.5 0.9 pad_maximum_fusion.2
  7.5 27.9 %all_gather.6 = bf16[336,512]{1,0:T(8,128)(2,1)S(1)} all-gather(bf16[168,512]{1,0:T(8,128)(2,1)S(1)} %pad_maximum_fusion.2), channel_id=1, replica_groups=mesh['y'=4,'x'=4,'zh'=2,'zl'=8,'core'=2] {'zh'}, dimensions={0}, use_global_device_ids=true | all-gather | bytes 516096 | tf_op jit(solution)/shard_map/all_gather | solution.py:44
  35.4 0.7 fusion.30
  36.1 0.0 all-gather.2.cloned.1.call-update
  36.1 1.7 %broadcast_in_dim.10 = bf16[16,336,256]{2,1,0:T(8,128)(2,1)} broadcast(bf16[336,256]{1,0:T(8,128)(2,1)S(1)} %get-tuple-element.8), dimensions={1,2} | broadcast | bytes 2924544 | tf_op jit(solution)/shard_map/broadcast_in_dim | solution.py:49
  37.8 7.3 %all-to-all-start = ((bf16[16,336,256]{2,1,0:T(8,128)(2,1)}), bf16[16,336,256]{2,1,0:T(8,128)(2,1)S(1)}, u32[]{:S(2)}, u32[]{:S(2)}) async-start(bf16[16,336,256]{2,1,0:T(8,128)(2,1)} %broadcast_in_dim.10), calls=%async_computation | async-start | bytes 5505024 | tf_op jit(solution)/shard_map/all_to_all | solution.py:48
  45.1 0.7 and_and_fusion
  45.8 36.0 %all-to-all-done = bf16[16,336,256]{2,1,0:T(8,128)(2,1)S(1)} async-done(((bf16[16,336,256]{2,1,0:T(8,128)(2,1)}), bf16[16,336,256]{2,1,0:T(8,128)(2,1)S(1)}, u32[]{:S(2)}, u32[]{:S(2)}) %all-to-all-start) | async-done | bytes 2752544 | tf_op jit(solution)/shard_map/all_to_all | solution.py:48
  81.8 0.0 copy-start.1
  81.8 3.8 %convolution_bitcast_fusion = f32[448,256]{1,0:T(8,128)S(1)} fusion(bf16[448,5376]{1,0:T(8,128)(2,1)} %param.6, bf16[5376,256]{1,0:T(8,128)(2,1)S(1)} %bitcast.52), kind=kOutput, calls=%fused_computation.10 | convolution fusion | flops 1233125376 | bytes 8028160 | tf_op jit(solution)/shard_map/dot_general | solution.py:54
  85.7 0.1 multiply_reduce_fusion.1
  85.8 0.0 copy-done.1
  85.8 0.1 multiply_bitcast_fusion
  86.0 1.1 fusion.17
  87.1 0.1 maximum_bitcast_fusion
  87.2 3.3 %collective-permute-start.1 = (bf16[448,256]{1,0:T(8,128)(2,1)S(1)}, bf16[448,256]{1,0:T(8,128)(2,1)S(1)}, u32[]{:S(2)}, u32[]{:S(2)}) collective-permute-start(bf16[448,256]{1,0:T(8,128)(2,1)S(1)} %pad_maximum_fusion), channel_id=1, source_target_pairs={{0,32},{16,48},{32,64},{48,80},{64,96},{80,112},{96,128},{112,144}... | collective-permute-start | bytes 688136 | tf_op jit(solution)/shard_map/ppermute | solution.py:34
  90.5 12.5 %collective-permute-start.2 = (bf16[448,256]{1,0:T(8,128)(2,1)S(1)}, bf16[448,256]{1,0:T(8,128)(2,1)S(1)}, u32[]{:S(2)}, u32[]{:S(2)}) collective-permute-start(bf16[448,256]{1,0:T(8,128)(2,1)S(1)} %pad_maximum_fusion), channel_id=1, source_target_pairs={{0,16},{16,32},{32,48},{48,64},{64,80},{80,96},{96,112},{112,128},... | collective-permute-start | bytes 688136 | tf_op jit(solution)/shard_map/ppermute | solution.py:34
  103.1 7.0 %collective-permute-start = (bf16[128,256]{1,0:T(8,128)(2,1)S(1)}, bf16[128,256]{1,0:T(8,128)(2,1)S(1)}, u32[]{:S(2)}, u32[]{:S(2)}) collective-permute-start(bf16[128,256]{1,0:T(8,128)(2,1)S(1)} %fusion.20), channel_id=1, source_target_pairs={{0,48},{16,64},{32,80},{48,96},{64,112},{80,128},{96,144},{112,160... | collective-permute-start | bytes 196616 | tf_op jit(solution)/shard_map/ppermute | solution.py:34
  110.1 0.9 multiply_cosine_fusion
  111.0 17.8 %collective-permute-done = bf16[128,256]{1,0:T(8,128)(2,1)S(1)} collective-permute-done((bf16[128,256]{1,0:T(8,128)(2,1)S(1)}, bf16[128,256]{1,0:T(8,128)(2,1)S(1)}, u32[]{:S(2)}, u32[]{:S(2)}) %collective-permute-start) | collective-permute-done | bytes 65568 | tf_op jit(solution)/shard_map/ppermute | solution.py:34
  128.8 0.0 collective-permute-done.1
  128.8 0.0 collective-permute-done.2
  128.8 0.1 maximum_maximum_fusion
  128.9 0.0 copy-start
  128.9 0.0 all-gather.2.cloned.1.call-done
  128.9 4.7 %fusion.32 = f32[256,448]{0,1:T(8,128)S(1)} fusion(bf16[448,5376]{1,0:T(8,128)(2,1)} %param.6, bf16[5376,256]{1,0:T(8,128)(2,1)} %all-gather.2.cloned.1.call-done), kind=kOutput, calls=%fused_computation.61 | convolution fusion | flops 1233125376 | bytes 8028160 | tf_op jit(solution)/shard_map/dot_general | solution.py:69
  133.6 0.2 reshape.229
  133.8 0.5 multiply_reduce_fusion
  134.4 0.1 copy.13
  134.5 0.0 copy-done
  134.5 0.2 fusion.10
  134.7 0.2 subtract_convert_fusion
  134.9 2.3 %fusion.31 = f32[2,448]{1,0:T(2,128)S(1)} fusion(pred[448,1472]{1,0:T(8,128)(4,1)S(1)} %and_and_fusion, bf16[1472,256]{1,0:T(8,128)(2,1)S(1)} %maximum_maximum_fusion, bf16[448,2,64]{2,0,1:T(8,128)(2,1)S(1)} %get-tuple-element.6, bf16[448,2,64]{2,0,1:T(8,128)(2,1)S(1)} %get-tuple-element.5), kind=kOutput, calls=%fused_computation.60 | convolution fusion | flops 343377344 | bytes 1527296 | tf_op jit(solution)/shard_map/sub | solution.py:89
  137.2 3.8 %fusion.7 = bf16[2,56,8,128]{3,2,1,0:T(8,128)(2,1)S(1)} fusion(f32[2,448]{1,0:T(2,128)S(1)} %fusion.31, bf16[1472,256]{1,0:T(8,128)(2,1)S(1)} %maximum_maximum_fusion, pred[448,1472]{1,0:T(8,128)(4,1)S(1)} %and_and_fusion, bf16[448,2,64]{2,0,1:T(8,128)(2,1)S(1)} %get-tuple-element.6, bf16[448,2,64]{2,0,1:T(8,128)(2,1)S(1)} %get-tuple-element.5), kind=kOutput, calls=%fused_computation.12 | convolution fusion | flops 682453312 | bytes 1875456 | tf_op jit(solution)/shard_map/gbc,cd->bgd/dot_general | solution.py:91
  141.0 0.7 copy.20
  (10 shorter events, 0.1 us)
Async XLA Ops:
  6.5 122.4 %all-gather.2.cloned.1.call-start = ((), (), s32[]{:S(2)}) async-start(), calls=%async_computation.1 | async-start | bytes 2924544 | tf_op jit(solution)/shard_map/all_gather | solution.py:47
  37.8 44.0 %all-to-all-start = ((bf16[16,336,256]{2,1,0:T(8,128)(2,1)}), bf16[16,336,256]{2,1,0:T(8,128)(2,1)S(1)}, u32[]{:S(2)}, u32[]{:S(2)}) async-start(bf16[16,336,256]{2,1,0:T(8,128)(2,1)} %broadcast_in_dim.10), calls=%async_computation | async-start | bytes 5505024 | tf_op jit(solution)/shard_map/all_to_all | solution.py:48
  81.8 4.0 %copy-start.1 = (f32[128]{0:T(128)S(1)}, f32[128]{0:T(128)}, u32[]{:S(2)}) copy-start(f32[128]{0:T(128)} %param.11) | copy-start | bytes 1540
  87.2 41.6 %collective-permute-start.1 = (bf16[448,256]{1,0:T(8,128)(2,1)S(1)}, bf16[448,256]{1,0:T(8,128)(2,1)S(1)}, u32[]{:S(2)}, u32[]{:S(2)}) collective-permute-start(bf16[448,256]{1,0:T(8,128)(2,1)S(1)} %pad_maximum_fusion), channel_id=1, source_target_pairs={{0,32},{16,48},{32,64},{48,80},{64,96},{80,112},{96,128},{112,144}... | collective-permute-start | bytes 688136 | tf_op jit(solution)/shard_map/ppermute | solution.py:34
  90.5 38.3 %collective-permute-start.2 = (bf16[448,256]{1,0:T(8,128)(2,1)S(1)}, bf16[448,256]{1,0:T(8,128)(2,1)S(1)}, u32[]{:S(2)}, u32[]{:S(2)}) collective-permute-start(bf16[448,256]{1,0:T(8,128)(2,1)S(1)} %pad_maximum_fusion), channel_id=1, source_target_pairs={{0,16},{16,32},{32,48},{48,64},{64,80},{80,96},{96,112},{112,128},... | collective-permute-start | bytes 688136 | tf_op jit(solution)/shard_map/ppermute | solution.py:34
  103.1 25.7 %collective-permute-start = (bf16[128,256]{1,0:T(8,128)(2,1)S(1)}, bf16[128,256]{1,0:T(8,128)(2,1)S(1)}, u32[]{:S(2)}, u32[]{:S(2)}) collective-permute-start(bf16[128,256]{1,0:T(8,128)(2,1)S(1)} %fusion.20), channel_id=1, source_target_pairs={{0,48},{16,64},{32,80},{48,96},{64,112},{80,128},{96,144},{112,160... | collective-permute-start | bytes 196616 | tf_op jit(solution)/shard_map/ppermute | solution.py:34
  128.9 5.6 %copy-start = (f32[128]{0:T(128)S(1)}, f32[128]{0:T(128)}, u32[]{:S(2)}) copy-start(f32[128]{0:T(128)} %param.10) | copy-start | bytes 1540
Sparse Core Ops, SparseCore 0:
  36.2 82.0 all-gather.1
where the time goes:
time: 149 us
  waiting for transfers between devices  53.9 us (36%)
  starting transfers between devices  30.1 us (20%)
  blocking collectives  27.9 us (19%)
  matrix products  14.5 us (10%)
  between operations  13.6 us (9%)
  other arithmetic  5.06 us (3%)
  local copies, waits for them, and re-layouts  3.53 us (2%)
    all_to_all x1, waiting for transfers between devices, on_device(): lax.all_to_all(jnp.broadcast_to(pair_kv[None], (plane,) + pair_kv.shape),...  36 us
    all_gather x1, blocking collectives, on_device(): pair = lax.all_gather(mine, 'zh', axis=0, tiled=True)  27.9 us
    ppermute x3, starting transfers between devices, from_behind(): lax.ppermute(block, CTX, [(i - distance, i) for i in range(distance, coun...  22.8 us
    ppermute x3, waiting for transfers between devices, from_behind(): lax.ppermute(block, CTX, [(i - distance, i) for i in range(distance, coun...  17.8 us
    all_to_all x1, starting transfers between devices, on_device(): lax.all_to_all(jnp.broadcast_to(pair_kv[None], (plane,) + pair_kv.shape),...  7.25 us
    dot_general x1, matrix products, on_device(): query_sum = jnp.dot(tokens, all_q, preferred_element_type=jnp.float32)  4.65 us
    dot_general x1, matrix products, on_device(): kv_sum = jnp.dot(tokens, all_kv, preferred_element_type=jnp.float32)  3.78 us
    dot_general x1, matrix products, on_device(): jnp.einsum('gbc,cd->bgd', probs, all_keys_values[:, head_size:], preferre...  3.76 us
  transfers between devices with their start and end apart: 5, of which 2 were waited for; matrix products, arithmetic and copies ran while one was open for 6% of the time, Pallas kernels for 0%

commit v1 on v0

--- a/solution.py
+++ b/solution.py
@@ -41,7 +41,9 @@
     q_width = w_query.shape[1]
     kv_width = 2 * head_size
     mine = jnp.concatenate([key_weight, value_weight, w_query], axis=1)
-    pair = lax.all_gather(mine, "zh", axis=0, tiled=True)
+    pair = jnp.concatenate(
+        lax.all_to_all(jnp.stack([mine] * lax.axis_size("zh")), "zh", 0, 0), axis=0
+    )
     pair_kv = pair[:, :kv_width]
     pair_q = pair[:, kv_width:]
     all_q = lax.all_gather(pair_q, PLANE, axis=0, tiled=True)

time: 149 us -> 156 us (1.047)
  the two profiles are of different devices: /device:TPU:50 before, /device:TPU:40 now
where the time goes in v1:
time: 156 us
  waiting for transfers between devices  55.7 us (36%)
  blocking collectives  39.8 us (26%)
  starting transfers between devices  23.6 us (15%)
  matrix products  14.5 us (9%)
  between operations  13.6 us (9%)
  other arithmetic  5.09 us (3%)
  local copies, waits for them, and re-layouts  3.53 us (2%)
    all_to_all x1, blocking collectives, on_device(): lax.all_to_all(jnp.stack([mine] * lax.axis_size('zh')), 'zh', 0, 0)  39.8 us
    all_to_all x1, waiting for transfers between devices, on_device(): lax.all_to_all(jnp.broadcast_to(pair_kv[None], (plane,) + pair_kv.shape),...  39.8 us
    ppermute x3, starting transfers between devices, from_behind(): lax.ppermute(block, CTX, [(i - distance, i) for i in range(distance, coun...  16.2 us
    ppermute x3, waiting for transfers between devices, from_behind(): lax.ppermute(block, CTX, [(i - distance, i) for i in range(distance, coun...  15.9 us
    all_to_all x1, starting transfers between devices, on_device(): lax.all_to_all(jnp.broadcast_to(pair_kv[None], (plane,) + pair_kv.shape),...  7.39 us
    dot_general x1, matrix products, on_device(): query_sum = jnp.dot(tokens, all_q, preferred_element_type=jnp.float32)  4.65 us
    dot_general x1, matrix products, on_device(): kv_sum = jnp.dot(tokens, all_kv, preferred_element_type=jnp.float32)  3.78 us
    dot_general x1, matrix products, on_device(): jnp.einsum('gbc,cd->bgd', probs, all_keys_values[:, head_size:], preferre...  3.76 us
  transfers between devices with their start and end apart: 5, of which 2 were waited for; matrix products, arithmetic and copies ran while one was open for 6% of the time, Pallas kernels for 0%

profile of v1, /device:TPU:40, one launch (start us, length us, event | category | flops | bytes accessed | tf_op | source)
XLA Modules:
  0.0 155.8 jit_solution(15544655499507934611)
XLA Ops:
  6.5 0.0 all-gather.2.cloned.1.call-start
  6.5 0.9 maximum_bitcast_fusion
  7.5 39.8 %all_to_all.10 = bf16[2,168,512]{2,1,0:T(8,128)(2,1)S(1)} all-to-all(bf16[2,168,512]{2,1,0:T(8,128)(2,1)S(1)} %pad_maximum_fusion), channel_id=1, replica_groups=mesh['y'=4,'x'=4,'zh'=2,'zl'=8,'core'=2] {'zh'}, dimensions={0} | all-to-all | bytes 688128 | tf_op jit(solution)/shard_map/all_to_all | solution.py:45
  47.3 0.7 fusion.30
  48.0 0.0 all-gather.2.cloned.1.call-update
  48.0 1.7 %broadcast_in_dim.10 = bf16[16,336,256]{2,1,0:T(8,128)(2,1)} broadcast(bf16[336,256]{1,0:T(8,128)(2,1)S(1)} %get-tuple-element.8), dimensions={1,2} | broadcast | bytes 2924544 | tf_op jit(solution)/shard_map/broadcast_in_dim | solution.py:51
  49.8 7.4 %all-to-all-start.1 = ((bf16[16,336,256]{2,1,0:T(8,128)(2,1)}), bf16[16,336,256]{2,1,0:T(8,128)(2,1)S(1)}, u32[]{:S(2)}, u32[]{:S(2)}) async-start(bf16[16,336,256]{2,1,0:T(8,128)(2,1)} %broadcast_in_dim.10), calls=%async_computation.1 | async-start | bytes 5505024 | tf_op jit(solution)/shard_map/all_to_all | solution.py:50
  57.2 0.7 and_and_fusion
  57.9 39.8 %all-to-all-done.1 = bf16[16,336,256]{2,1,0:T(8,128)(2,1)S(1)} async-done(((bf16[16,336,256]{2,1,0:T(8,128)(2,1)}), bf16[16,336,256]{2,1,0:T(8,128)(2,1)S(1)}, u32[]{:S(2)}, u32[]{:S(2)}) %all-to-all-start.1) | async-done | bytes 2752544 | tf_op jit(solution)/shard_map/all_to_all | solution.py:50
  97.7 0.0 copy-start.1
  97.7 3.8 %convolution_bitcast_fusion = f32[448,256]{1,0:T(8,128)S(1)} fusion(bf16[448,5376]{1,0:T(8,128)(2,1)} %param.6, bf16[5376,256]{1,0:T(8,128)(2,1)S(1)} %bitcast.55), kind=kOutput, calls=%fused_computation.10 | convolution fusion | flops 1233125376 | bytes 8028160 | tf_op jit(solution)/shard_map/dot_general | solution.py:56
  101.5 0.1 multiply_reduce_fusion.1
  101.7 0.0 copy-done.1
  101.7 0.1 multiply_bitcast_fusion
  101.8 1.1 fusion.17
  102.9 0.1 maximum_bitcast_fusion.1
  103.1 1.9 %collective-permute-start.1 = (bf16[448,256]{1,0:T(8,128)(2,1)S(1)}, bf16[448,256]{1,0:T(8,128)(2,1)S(1)}, u32[]{:S(2)}, u32[]{:S(2)}) collective-permute-start(bf16[448,256]{1,0:T(8,128)(2,1)S(1)} %pad_maximum_fusion.1), channel_id=1, source_target_pairs={{0,32},{16,48},{32,64},{48,80},{64,96},{80,112},{96,128},{112,144}... | collective-permute-start | bytes 688136 | tf_op jit(solution)/shard_map/ppermute | solution.py:34
  105.0 1.9 %collective-permute-start.2 = (bf16[448,256]{1,0:T(8,128)(2,1)S(1)}, bf16[448,256]{1,0:T(8,128)(2,1)S(1)}, u32[]{:S(2)}, u32[]{:S(2)}) collective-permute-start(bf16[448,256]{1,0:T(8,128)(2,1)S(1)} %pad_maximum_fusion.1), channel_id=1, source_target_pairs={{0,16},{16,32},{32,48},{48,64},{64,80},{80,96},{96,112},{112,128},... | collective-permute-start | bytes 688136 | tf_op jit(solution)/shard_map/ppermute | solution.py:34
  106.9 12.3 %collective-permute-start = (bf16[128,256]{1,0:T(8,128)(2,1)S(1)}, bf16[128,256]{1,0:T(8,128)(2,1)S(1)}, u32[]{:S(2)}, u32[]{:S(2)}) collective-permute-start(bf16[128,256]{1,0:T(8,128)(2,1)S(1)} %fusion.20), channel_id=1, source_target_pairs={{0,48},{16,64},{32,80},{48,96},{64,112},{80,128},{96,144},{112,160... | collective-permute-start | bytes 196616 | tf_op jit(solution)/shard_map/ppermute | solution.py:34
  119.3 0.9 multiply_cosine_fusion
  120.1 15.9 %collective-permute-done = bf16[128,256]{1,0:T(8,128)(2,1)S(1)} collective-permute-done((bf16[128,256]{1,0:T(8,128)(2,1)S(1)}, bf16[128,256]{1,0:T(8,128)(2,1)S(1)}, u32[]{:S(2)}, u32[]{:S(2)}) %collective-permute-start) | collective-permute-done | bytes 65568 | tf_op jit(solution)/shard_map/ppermute | solution.py:34
  136.0 0.0 collective-permute-done.1
  136.0 0.0 collective-permute-done.2
  136.0 0.1 maximum_maximum_fusion
  136.1 0.0 copy-start
  136.1 0.0 all-gather.2.cloned.1.call-done
  136.1 4.7 %fusion.32 = f32[256,448]{0,1:T(8,128)S(1)} fusion(bf16[448,5376]{1,0:T(8,128)(2,1)} %param.6, bf16[5376,256]{1,0:T(8,128)(2,1)} %all-gather.2.cloned.1.call-done), kind=kOutput, calls=%fused_computation.62 | convolution fusion | flops 1233125376 | bytes 8028160 | tf_op jit(solution)/shard_map/dot_general | solution.py:71
  140.8 0.2 reshape.233
  141.0 0.5 multiply_reduce_fusion
  141.6 0.1 copy.13
  141.7 0.0 copy-done
  141.7 0.2 fusion.10
  141.9 0.2 subtract_convert_fusion
  142.1 2.3 %fusion.31 = f32[2,448]{1,0:T(2,128)S(1)} fusion(pred[448,1472]{1,0:T(8,128)(4,1)S(1)} %and_and_fusion, bf16[1472,256]{1,0:T(8,128)(2,1)S(1)} %maximum_maximum_fusion, bf16[448,2,64]{2,0,1:T(8,128)(2,1)S(1)} %get-tuple-element.6, bf16[448,2,64]{2,0,1:T(8,128)(2,1)S(1)} %get-tuple-element.5), kind=kOutput, calls=%fused_computation.61 | convolution fusion | flops 343377344 | bytes 1527296 | tf_op jit(solution)/shard_map/sub | solution.py:91
  144.4 3.8 %fusion.7 = bf16[2,56,8,128]{3,2,1,0:T(8,128)(2,1)S(1)} fusion(f32[2,448]{1,0:T(2,128)S(1)} %fusion.31, bf16[1472,256]{1,0:T(8,128)(2,1)S(1)} %maximum_maximum_fusion, pred[448,1472]{1,0:T(8,128)(4,1)S(1)} %and_and_fusion, bf16[448,2,64]{2,0,1:T(8,128)(2,1)S(1)} %get-tuple-element.6, bf16[448,2,64]{2,0,1:T(8,128)(2,1)S(1)} %get-tuple-element.5), kind=kOutput, calls=%fused_computation.12 | convolution fusion | flops 682453312 | bytes 1875456 | tf_op jit(solution)/shard_map/gbc,cd->bgd/dot_general | solution.py:93
  148.2 0.7 copy.20
  (11 shorter events, 0.1 us)
Async XLA Ops:
  6.5 129.6 %all-gather.2.cloned.1.call-start = ((), (), s32[]{:S(2)}) async-start(), calls=%async_computation.2 | async-start | bytes 2924544 | tf_op jit(solution)/shard_map/all_gather | solution.py:49
  49.8 47.9 %all-to-all-start.1 = ((bf16[16,336,256]{2,1,0:T(8,128)(2,1)}), bf16[16,336,256]{2,1,0:T(8,128)(2,1)S(1)}, u32[]{:S(2)}, u32[]{:S(2)}) async-start(bf16[16,336,256]{2,1,0:T(8,128)(2,1)} %broadcast_in_dim.10), calls=%async_computation.1 | async-start | bytes 5505024 | tf_op jit(solution)/shard_map/all_to_all | solution.py:50
  97.7 4.0 %copy-start.1 = (f32[128]{0:T(128)S(1)}, f32[128]{0:T(128)}, u32[]{:S(2)}) copy-start(f32[128]{0:T(128)} %param.11) | copy-start | bytes 1540
  103.1 33.0 %collective-permute-start.1 = (bf16[448,256]{1,0:T(8,128)(2,1)S(1)}, bf16[448,256]{1,0:T(8,128)(2,1)S(1)}, u32[]{:S(2)}, u32[]{:S(2)}) collective-permute-start(bf16[448,256]{1,0:T(8,128)(2,1)S(1)} %pad_maximum_fusion.1), channel_id=1, source_target_pairs={{0,32},{16,48},{32,64},{48,80},{64,96},{80,112},{96,128},{112,144}... | collective-permute-start | bytes 688136 | tf_op jit(solution)/shard_map/ppermute | solution.py:34
  105.0 31.0 %collective-permute-start.2 = (bf16[448,256]{1,0:T(8,128)(2,1)S(1)}, bf16[448,256]{1,0:T(8,128)(2,1)S(1)}, u32[]{:S(2)}, u32[]{:S(2)}) collective-permute-start(bf16[448,256]{1,0:T(8,128)(2,1)S(1)} %pad_maximum_fusion.1), channel_id=1, source_target_pairs={{0,16},{16,32},{32,48},{48,64},{64,80},{80,96},{96,112},{112,128},... | collective-permute-start | bytes 688136 | tf_op jit(solution)/shard_map/ppermute | solution.py:34
  106.9 29.1 %collective-permute-start = (bf16[128,256]{1,0:T(8,128)(2,1)S(1)}, bf16[128,256]{1,0:T(8,128)(2,1)S(1)}, u32[]{:S(2)}, u32[]{:S(2)}) collective-permute-start(bf16[128,256]{1,0:T(8,128)(2,1)S(1)} %fusion.20), channel_id=1, source_target_pairs={{0,48},{16,64},{32,80},{48,96},{64,112},{80,128},{96,144},{112,160... | collective-permute-start | bytes 196616 | tf_op jit(solution)/shard_map/ppermute | solution.py:34
  136.1 5.6 %copy-start = (f32[128]{0:T(128)S(1)}, f32[128]{0:T(128)}, u32[]{:S(2)}) copy-start(f32[128]{0:T(128)} %param.10) | copy-start | bytes 1540
Sparse Core Ops, SparseCore 0:
  48.1 73.3 all-gather.1
